TPU v7x, 512 devices: a whole 4x4x16 slice. The times are simulated.
512 devices in a mesh: rep: 4 (over x), fsdp: 16 (over z), tp: 8 (over y, core).
Axes of the slice: x: 4, y: 4, z: 16, core: 2. Of those that a mesh axis runs over, the one named last changes fastest.
Arguments:
- tracker: bfloat16 [4, 4096, 14336], P('rep', 'fsdp', 'tp'), may hold values from -20 to 20
- grad_delta: bfloat16 [4, 4096, 14336], P('rep', 'fsdp', 'tp'), may hold values from -20 to 20
- momentum: bfloat16 [4, 4096, 14336], P('rep', 'fsdp', 'tp'), may hold values from -20 to 20
- q_basis: bfloat16 [4, 14336, 512], P('rep', 'tp', 'fsdp'), may hold values from -0.046875 to 0.046875
- mix_counts: int32 [4, 3], replicated, may hold values from 1 to 8
Outputs:
- new_tracker: bfloat16 [4, 4096, 14336], P('rep', 'fsdp', 'tp')
- new_momentum: bfloat16 [4, 4096, 14336], P('rep', 'fsdp', 'tp')
- left_basis: bfloat16 [4, 4096, 512], P('rep', 'fsdp')
- q_new: bfloat16 [4, 14336, 512], P('rep', 'tp', 'fsdp')
All inputs are finite; a program needn't handle non-finite values.
Results may differ from a plain program's by a relative error of at most 0.0061.
Values may be sent and summed in bfloat16 or wider, within the bound.
A program may use at most 64 MiB of HBM per device.

v0:
```python
import jax
import jax.numpy as jnp
from jax import lax
from jax.sharding import PartitionSpec as P

D = 4096
FF = 14336


def extended(block, sides, width):
    for axis, dim in sides:
        count = lax.axis_size(axis)
        forward = [(i, i + 1) for i in range(count - 1)]
        forward.append((count - 1, 0))
        backward = [(target, source) for source, target in forward]
        low = lax.ppermute(
            lax.slice_in_dim(block, block.shape[dim] - width, None, axis=dim), axis, forward
        )
        high = lax.ppermute(lax.slice_in_dim(block, 0, width, axis=dim), axis, backward)
        block = jnp.concatenate([low, block, high], axis=dim)
    return block


def orthonormal(pmat, gram):
    factor = jnp.linalg.cholesky(gram)
    solved = jax.scipy.linalg.solve_triangular(factor, pmat.T, lower=True).T
    return (solved * jnp.sqrt(jnp.float32(D))).astype(jnp.bfloat16)


def local(tracker, grad_delta, momentum, q_basis, mix_counts):
    agent = lax.axis_index("rep")
    counts = mix_counts.astype(jnp.float32)
    select = (jnp.arange(counts.shape[0]) == agent).astype(jnp.float32)
    mine = jnp.sum(select[:, None] * counts, axis=0)
    weights = mine / jnp.sum(mine)
    near = extended(tracker, (("rep", 0),), 1)
    mixed = (
        weights[0] * near[1].astype(jnp.float32)
        + weights[1] * near[0].astype(jnp.float32)
        + weights[2] * near[2].astype(jnp.float32)
    )
    tracked = mixed + grad_delta[0].astype(jnp.float32)
    new_tracker = tracked.astype(jnp.bfloat16)
    accum = momentum[0].astype(jnp.float32) + tracked
    accum_b = accum.astype(jnp.bfloat16)
    scale = 1.0 / jnp.sqrt(jnp.float32(D))
    basis_full = lax.all_gather(q_basis, "fsdp", axis=2, tiled=True)[0]
    partial_left = jnp.dot(accum_b, basis_full, preferred_element_type=jnp.float32)
    pmat = lax.psum(partial_left, "tp")
    gram_part = jnp.dot(pmat.T, pmat, precision=lax.Precision.HIGHEST)
    gram = lax.psum(gram_part, "fsdp")
    left_b = orthonormal(pmat, gram)
    block = left_b
    product = lax.dot_general(
        block, accum_b, (((0,), (0,)), ((), ())), preferred_element_type=jnp.float32
    )
    right_t = lax.psum_scatter(product * scale, "fsdp", scatter_dimension=0, tiled=True)
    squares = lax.psum(jnp.sum(right_t * right_t, axis=1), "tp")
    rms = jnp.sqrt(squares / FF) + 1e-06
    q_new = (right_t / rms[:, None]).T.astype(jnp.bfloat16)
    right_b = right_t.astype(jnp.bfloat16)
    block = left_b
    feed = jnp.dot(
        block,
        lax.all_gather(right_b, "fsdp", axis=0, tiled=True),
        preferred_element_type=jnp.float32,
    )
    new_momentum = (accum - 0.5 * scale * feed).astype(jnp.bfloat16)
    return (new_tracker[None], new_momentum[None], left_b[None], q_new[None])


def solution(mesh):
    in_specs = (
        P("rep", "fsdp", "tp"),
        P("rep", "fsdp", "tp"),
        P("rep", "fsdp", "tp"),
        P("rep", "tp", "fsdp"),
        P(),
    )
    out_specs = (
        P("rep", "fsdp", "tp"),
        P("rep", "fsdp", "tp"),
        P("rep", "fsdp", None),
        P("rep", "tp", "fsdp"),
    )
    return jax.shard_map(local, mesh=mesh, in_specs=in_specs, out_specs=out_specs, check_vma=False)
```

profile of v0, /device:TPU:2, one launch (start us, length us, event | category | flops | bytes accessed | tf_op | source)
XLA Modules:
  0.0 640.5 jit_solution(14598845073682928262)
XLA Ops:
  7.9 7.8 %collective-permute-start.1 = (bf16[1,256,1792]{2,1,0:T(8,128)(2,1)}, bf16[1,256,1792]{2,1,0:T(8,128)(2,1)S(1)}, u32[]{:S(2)}, u32[]{:S(2)}) collective-permute-start(bf16[1,256,1792]{2,1,0:T(8,128)(2,1)} %param.5), channel_id=1, source_target_pairs={{128,0},{256,128},{384,256},{0,384},{129,1},{257,129},{385,257},{1... | collective-permute-start | bytes 2752520 | tf_op jit(solution)/shard_map/ppermute | solution.py:19
  15.8 1.9 collective-permute-start
  20.3 11.8 %collective-permute-done.1 = bf16[1,256,1792]{2,1,0:T(8,128)(2,1)S(1)} collective-permute-done((bf16[1,256,1792]{2,1,0:T(8,128)(2,1)}, bf16[1,256,1792]{2,1,0:T(8,128)(2,1)S(1)}, u32[]{:S(2)}, u32[]{:S(2)}) %collective-permute-start.1) | collective-permute-done | bytes 917536 | tf_op jit(solution)/shard_map/ppermute | solution.py:19
  32.1 3.2 collective-permute-done
  36.3 5.5 fusion.44
  41.8 45.7 %all-gather.3.cloned.1.call-done = bf16[1,1792,512]{1,2,0:T(8,128)(2,1)} async-done(((bf16[1,1792,32]{1,2,0:T(8,128)(2,1)}), bf16[1,1792,512]{1,2,0:T(8,128)(2,1)}) %all-gather.3.cloned.1.call-update) | async-done | bytes 1835024 | tf_op jit(solution)/shard_map/all_gather | solution.py:47
  87.5 3.0 fusion.3
  90.6 73.0 %all-reduce.4.cloned.1.call-done = f32[256,512]{1,0:T(8,128)} async-done(((f32[256,512]{1,0:T(8,128)}), f32[256,512]{1,0:T(8,128)}) %all-reduce.4.cloned.1.call-update) | async-done | bytes 524304 | tf_op jit(solution)/shard_map/psum | solution.py:49
  163.6 3.3 fusion.47
  167.1 138.0 %all-reduce.6.cloned.1.call-done = f32[512,512]{0,1:T(8,128)} async-done(((f32[512,512]{0,1:T(8,128)}), f32[512,512]{0,1:T(8,128)}) %all-reduce.6.cloned.1.call-update) | async-done | bytes 1048592 | tf_op jit(solution)/shard_map/psum | solution.py:51
  305.1 2.6 copy.10
  310.5 11.7 %cholesky.104 = f32[128,128]{1,0:T(8,128)S(1)} custom-call(f32[128,128]{1,0:T(8,128)S(1)} %cholesky.266), custom_call_target="Cholesky" | custom-call | tf_op jit(solution)/shard_map/jit(cholesky)/cholesky | solution.py:25
  323.4 9.8 %custom-call.31 = f32[1,128,128]{1,2,0:T(8,128)S(1)} custom-call(f32[1,128,128]{2,1,0:T(8,128)S(1)} %get-tuple-element.41), custom_call_target="InvertDiagBlocksLowerTriangular" | custom-call | tf_op jit(solution)/shard_map/jit(cholesky)/cholesky | solution.py:25
  333.2 2.0 constant_dynamic-update-slice_fusion.3
  336.5 11.7 %cholesky.217 = f32[128,128]{1,0:T(8,128)S(1)} custom-call(f32[128,128]{1,0:T(8,128)S(1)} %cholesky.270), custom_call_target="Cholesky" | custom-call | tf_op jit(solution)/shard_map/jit(cholesky)/cholesky | solution.py:25
  348.8 10.0 %custom-call.32 = f32[1,128,128]{1,2,0:T(8,128)S(1)} custom-call(f32[1,128,128]{2,1,0:T(8,128)S(1)} %get-tuple-element.38), custom_call_target="InvertDiagBlocksLowerTriangular" | custom-call | tf_op jit(solution)/shard_map/jit(cholesky)/cholesky | solution.py:25
  361.2 11.7 %cholesky.238 = f32[128,128]{1,0:T(8,128)S(1)} custom-call(f32[128,128]{1,0:T(8,128)S(1)} %cholesky.275), custom_call_target="Cholesky" | custom-call | tf_op jit(solution)/shard_map/jit(cholesky)/cholesky | solution.py:25
  373.6 9.8 %custom-call.33 = f32[1,128,128]{1,2,0:T(8,128)S(1)} custom-call(f32[1,128,128]{2,1,0:T(8,128)S(1)} %get-tuple-element.35), custom_call_target="InvertDiagBlocksLowerTriangular" | custom-call | tf_op jit(solution)/shard_map/jit(cholesky)/cholesky | solution.py:25
  385.6 11.7 %cholesky.255 = f32[128,128]{1,0:T(8,128)S(1)} custom-call(f32[128,128]{1,0:T(8,128)S(1)} %convolution_subtract_fusion.5), custom_call_target="Cholesky" | custom-call | tf_op jit(solution)/shard_map/jit(cholesky)/cholesky | solution.py:25
  402.5 2.6 select_select_fusion
  405.1 14.5 %while.1 = (s32[]{:T(128)}, f32[512,512]{1,0:T(8,128)}, s32[4,2]{0,1:T(2,128)S(1)}, f32[4,128,128]{2,1,0:T(8,128)}, s32[]{:T(128)}) while((s32[]{:T(128)}, f32[512,512]{1,0:T(8,128)}, s32[4,2]{0,1:T(2,128)S(1)}, f32[4,128,128]{2,1,0:T(8,128)}, s32[]{:T(128)}) %tuple.37), condition=%wide.while_cond, body=%wide.while_body.sunk | while | flops 2 | bytes 132205 | solution.py:26
  405.8 3.0 bitcast_dynamic-update-slice_fusion.2
  409.4 3.0 bitcast_dynamic-update-slice_fusion.2
  413.1 3.0 bitcast_dynamic-update-slice_fusion.2
  416.7 2.9 bitcast_dynamic-update-slice_fusion.2
  419.6 40.8 %custom-call.34 = f32[4,128,128]{1,2,0:T(8,128)} custom-call(f32[4,128,128]{2,1,0:T(8,128)} %get-tuple-element.11), custom_call_target="InvertDiagBlocksLowerTriangular" | custom-call | tf_op jit(solution)/shard_map/jit(_solve_triangular)/triangular_solve | solution.py:26
  466.6 1.8 convolution_subtract_fusion.1
  469.6 2.5 convolution_multiply_fusion
  472.1 75.2 %reduce-scatter.2.cloned.1.call-done = f32[32,1792]{1,0:T(8,128)} async-done(((f32[512,1792]{1,0:T(8,128)}), f32[32,1792]{1,0:T(8,128)}) %reduce-scatter.2.cloned.1.call-update) | async-done | bytes 229392 | tf_op jit(solution)/shard_map/reduce_scatter | solution.py:57
  548.4 12.4 %psum.23 = f32[32]{0:T(128)S(1)} all-reduce(f32[32]{0:T(128)S(1)} %multiply_reduce_fusion), channel_id=1, replica_groups=mesh['rep'=4,'fsdp'=16,'tp'=8] {'tp'}, use_global_device_ids=true, to_apply=%region_14.15 | all-reduce | flops 32 | bytes 256 | tf_op jit(solution)/shard_map/psum | solution.py:58
  563.5 67.4 %all-gather.5.cloned.1.call-done = bf16[512,1792]{1,0:T(8,128)(2,1)} async-done(((bf16[32,1792]{1,0:T(8,128)(2,1)}), bf16[512,1792]{1,0:T(8,128)(2,1)}) %all-gather.5.cloned.1.call-update) | async-done | bytes 1835024 | tf_op jit(solution)/shard_map/all_gather | solution.py:65
  630.9 3.1 fusion.2
  (67 shorter events, 32.2 us)
Async XLA Ops:
  7.2 80.3 %all-gather.3.cloned.1.call-start = ((), (), s32[]{:S(2)}) async-start(), calls=%async_computation.1 | async-start | bytes 1949696 | tf_op jit(solution)/shard_map/all_gather | solution.py:47
  7.9 155.7 %all-reduce.4.cloned.1.call-start = ((), (), s32[]{:S(2)}) async-start(), calls=%async_computation.2 | async-start | bytes 1048576 | tf_op jit(solution)/shard_map/psum | solution.py:49
  7.9 24.2 %collective-permute-start.1 = (bf16[1,256,1792]{2,1,0:T(8,128)(2,1)}, bf16[1,256,1792]{2,1,0:T(8,128)(2,1)S(1)}, u32[]{:S(2)}, u32[]{:S(2)}) collective-permute-start(bf16[1,256,1792]{2,1,0:T(8,128)(2,1)} %param.5), channel_id=1, source_target_pairs={{128,0},{256,128},{384,256},{0,384},{129,1},{257,129},{385,257},{1... | collective-permute-start | bytes 2752520 | tf_op jit(solution)/shard_map/ppermute | solution.py:19
  15.8 19.6 %collective-permute-start = (bf16[1,256,1792]{2,1,0:T(8,128)(2,1)}, bf16[1,256,1792]{2,1,0:T(8,128)(2,1)S(1)}, u32[]{:S(2)}, u32[]{:S(2)}) collective-permute-start(bf16[1,256,1792]{2,1,0:T(8,128)(2,1)} %param.5), channel_id=1, source_target_pairs={{0,128},{128,256},{256,384},{384,0},{1,129},{129,257},{257,385},{3... | collective-permute-start | bytes 2752520 | tf_op jit(solution)/shard_map/ppermute | solution.py:16
  32.1 3.2 copy-start.5
  35.3 0.9 copy-start.6
  36.3 51.2 %copy-start = (bf16[1,256,1792]{2,1,0:T(8,128)(2,1)S(1)}, bf16[1,256,1792]{2,1,0:T(8,128)(2,1)}, u32[]{:S(2)}) copy-start(bf16[1,256,1792]{2,1,0:T(8,128)(2,1)} %param.7) | copy-start | bytes 2752516
  90.5 214.6 %all-reduce.6.cloned.1.call-start = ((), (), s32[]{:S(2)}) async-start(), calls=%async_computation.3 | async-start | bytes 2097152 | tf_op jit(solution)/shard_map/psum | solution.py:51
  166.9 380.4 %reduce-scatter.2.cloned.1.call-start = ((), (), s32[]{:S(2)}) async-start(), calls=%async_computation.4 | async-start | bytes 3899392 | tf_op jit(solution)/shard_map/reduce_scatter | solution.py:57
  309.5 1.0 copy-start.4
  373.6 86.8 %copy-start.1 = (f32[256,512]{1,0:T(8,128)S(1)}, f32[256,512]{1,0:T(8,128)}, u32[]{:S(2)}) copy-start(f32[256,512]{1,0:T(8,128)} %all-reduce.4.cloned.1.call-done) | copy-start | bytes 1572868
  466.6 3.0 copy-start.2
  472.0 90.6 %copy-start.3 = (f32[128,256]{1,0:T(8,128)S(1)}, f32[128,256]{1,0:T(8,128)}, u32[]{:S(2)}) copy-start(f32[128,256]{1,0:T(8,128)} %copy-done.2) | copy-start | bytes 393220
  472.1 158.8 %all-gather.5.cloned.1.call-start = ((), (), s32[]{:S(2)}) async-start(), calls=%async_computation.5 | async-start | bytes 1949696 | tf_op jit(solution)/shard_map/all_gather | solution.py:65
Sparse Core Ops, SparseCore 0:
  10.1 77.3 all-gather.2
  90.6 72.8 all-reduce.3
  167.0 138.0 all-reduce.5
  472.2 75.0 reduce-scatter.1
  562.7 68.1 all-gather.4
where the time goes:
time: 642 us; the launch traced here: 641 us
  waiting for transfers between devices  415 us (65%)
  other arithmetic  136 us (21%)
  matrix products  28.8 us (4%)
  local copies, waits for them, and re-layouts  21.6 us (3%)
  between operations  16.5 us (3%)
  blocking collectives  12.4 us (2%)
  starting transfers between devices  10.1 us (2%)
    psum x1, waiting for transfers between devices, local(): gram = lax.psum(gram_part, 'fsdp')  138 us
    another operation x14, other arithmetic, orthonormal(): factor = jnp.linalg.cholesky(gram)  80.4 us
    reduce_scatter x1, waiting for transfers between devices, local(): lax.psum_scatter(product * scale, 'fsdp', scatter_dimension=0, tiled=True)  75.2 us
    psum x1, waiting for transfers between devices, local(): pmat = lax.psum(partial_left, 'tp')  73 us
    all_gather x1, waiting for transfers between devices, local(): lax.all_gather(right_b, 'fsdp', axis=0, tiled=True)  67.4 us
    all_gather x1, waiting for transfers between devices, local(): basis_full = lax.all_gather(q_basis, 'fsdp', axis=2, tiled=True)[0]  45.7 us
    another operation x3, other arithmetic, orthonormal(): solved = jax.scipy.linalg.solve_triangular(factor, pmat.T, lower=True).T  43.4 us
    another operation x12, local copies, waits for them, and re-layouts  14.5 us
  transfers between devices with their start and end apart: 7, of which 7 were waited for; matrix products, arithmetic and copies ran while one was open for 1% of the time, Pallas kernels for 0%

commit v1 on v0

--- a/solution.py
+++ b/solution.py
@@ -5,6 +5,15 @@
 
 D = 4096
 FF = 14336
+
+
+def sum_by_hops(x, name):
+    peers = lax.axis_size(name)
+    result, stride = (x, 1)
+    while stride < peers:
+        result = result + lax.ppermute(result, name, [(i, i ^ stride) for i in range(peers)])
+        stride = 2 * stride
+    return result
 
 
 def extended(block, sides, width):
@@ -48,7 +57,7 @@
     partial_left = jnp.dot(accum_b, basis_full, preferred_element_type=jnp.float32)
     pmat = lax.psum(partial_left, "tp")
     gram_part = jnp.dot(pmat.T, pmat, precision=lax.Precision.HIGHEST)
-    gram = lax.psum(gram_part, "fsdp")
+    gram = sum_by_hops(gram_part, "fsdp")
     left_b = orthonormal(pmat, gram)
     block = left_b
     product = lax.dot_general(

time: 642 us -> 771 us (1.20)
  waiting for transfers between devices: 415 us -> 522 us
  starting transfers between devices: 10.1 us -> 37.1 us
    ppermute x0 -> x4, waiting for transfers between devices: none -> 220 us  [sum_by_hops(): lax.ppermute(result, name, [(i, i ^ stride) for i in range(peers)])]
    psum x1 -> x0, waiting for transfers between devices: 138 us -> none  [local(): gram = lax.psum(gram_part, 'fsdp')]
    ppermute x0 -> x4, starting transfers between devices: none -> 27.2 us  [sum_by_hops(): lax.ppermute(result, name, [(i, i ^ stride) for i in range(peers)])]
    reduce_scatter x1, waiting for transfers between devices: 75.2 us -> 99.6 us  [local(): lax.psum_scatter(product * scale, 'fsdp', scatter_dimension=0, tiled=True)]
  transfers between devices with their start and end apart: 7 -> 10, of which waited for: 7 -> 10; matrix products, arithmetic and copies ran while one was open for 1% -> 1% of each run, Pallas kernels for 0% -> 0%
where the time goes in v1:
time: 771 us; the launch traced here: 770 us
  waiting for transfers between devices  522 us (68%)
  other arithmetic  137 us (18%)
  starting transfers between devices  37.1 us (5%)
  matrix products  26.2 us (3%)
  local copies, waits for them, and re-layouts  18.9 us (2%)
  between operations  16.6 us (2%)
  blocking collectives  12.4 us (2%)
    ppermute x4, waiting for transfers between devices, sum_by_hops(): lax.ppermute(result, name, [(i, i ^ stride) for i in range(peers)])  220 us
    reduce_scatter x1, waiting for transfers between devices, local(): lax.psum_scatter(product * scale, 'fsdp', scatter_dimension=0, tiled=True)  99.6 us
    another operation x14, other arithmetic, orthonormal(): factor = jnp.linalg.cholesky(gram)  81 us
    psum x1, waiting for transfers between devices, local(): pmat = lax.psum(partial_left, 'tp')  73 us
    all_gather x1, waiting for transfers between devices, local(): lax.all_gather(right_b, 'fsdp', axis=0, tiled=True)  67.5 us
    all_gather x1, waiting for transfers between devices, local(): basis_full = lax.all_gather(q_basis, 'fsdp', axis=2, tiled=True)[0]  45.7 us
    another operation x3, other arithmetic, orthonormal(): solved = jax.scipy.linalg.solve_triangular(factor, pmat.T, lower=True).T  42 us
    ppermute x4, starting transfers between devices, sum_by_hops(): lax.ppermute(result, name, [(i, i ^ stride) for i in range(peers)])  27.2 us
  transfers between devices with their start and end apart: 10, of which 10 were waited for; matrix products, arithmetic and copies ran while one was open for 1% of the time, Pallas kernels for 0%

profile of v1, /device:TPU:2, one launch (start us, length us, event | category | flops | bytes accessed | tf_op | source)
XLA Modules:
  0.0 770.2 jit_solution(9823541892567727847)
XLA Ops:
  7.9 7.8 %collective-permute-start.1 = (bf16[1,256,1792]{2,1,0:T(8,128)(2,1)}, bf16[1,256,1792]{2,1,0:T(8,128)(2,1)S(1)}, u32[]{:S(2)}, u32[]{:S(2)}) collective-permute-start(bf16[1,256,1792]{2,1,0:T(8,128)(2,1)} %param.5), channel_id=1, source_target_pairs={{128,0},{256,128},{384,256},{0,384},{129,1},{257,129},{385,257},{1... | collective-permute-start | bytes 2752520 | tf_op jit(solution)/shard_map/ppermute | solution.py:28
  20.3 11.8 %collective-permute-done.1 = bf16[1,256,1792]{2,1,0:T(8,128)(2,1)S(1)} collective-permute-done((bf16[1,256,1792]{2,1,0:T(8,128)(2,1)}, bf16[1,256,1792]{2,1,0:T(8,128)(2,1)S(1)}, u32[]{:S(2)}, u32[]{:S(2)}) %collective-permute-start.1) | collective-permute-done | bytes 917536 | tf_op jit(solution)/shard_map/ppermute | solution.py:28
  32.1 3.2 collective-permute-done
  36.3 5.5 fusion.49
  41.8 45.7 %all-gather.3.cloned.1.call-done = bf16[1,1792,512]{1,2,0:T(8,128)(2,1)} async-done(((bf16[1,1792,32]{1,2,0:T(8,128)(2,1)}), bf16[1,1792,512]{1,2,0:T(8,128)(2,1)}) %all-gather.3.cloned.1.call-update) | async-done | bytes 1835024 | tf_op jit(solution)/shard_map/all_gather | solution.py:56
  87.5 3.0 fusion.3
  90.6 73.0 %all-reduce.3.cloned.1.call-done = f32[256,512]{1,0:T(8,128)} async-done(((f32[256,512]{1,0:T(8,128)}), f32[256,512]{1,0:T(8,128)}) %all-reduce.3.cloned.1.call-update) | async-done | bytes 524304 | tf_op jit(solution)/shard_map/psum | solution.py:58
  165.8 3.5 collective-permute-start.2
  169.3 21.3 %collective-permute-done.2 = f32[512,512]{0,1:T(8,128)S(1)} collective-permute-done((f32[512,512]{0,1:T(8,128)S(1)}, f32[512,512]{0,1:T(8,128)S(1)}, u32[]{:S(2)}, u32[]{:S(2)}) %collective-permute-start.2) | collective-permute-done | bytes 1048608 | tf_op jit(solution)/shard_map/ppermute | solution.py:14
  190.8 4.5 collective-permute-start.3
  195.3 42.7 %collective-permute-done.3 = f32[512,512]{0,1:T(8,128)S(1)} collective-permute-done((f32[512,512]{0,1:T(8,128)S(1)}, f32[512,512]{0,1:T(8,128)S(1)}, u32[]{:S(2)}, u32[]{:S(2)}) %collective-permute-start.3) | collective-permute-done | bytes 1048608 | tf_op jit(solution)/shard_map/ppermute | solution.py:14
  238.2 7.6 collective-permute-start.4
  245.9 111.5 %collective-permute-done.4 = f32[512,512]{0,1:T(8,128)S(1)} collective-permute-done((f32[512,512]{0,1:T(8,128)S(1)}, f32[512,512]{0,1:T(8,128)S(1)}, u32[]{:S(2)}, u32[]{:S(2)}) %collective-permute-start.4) | collective-permute-done | bytes 1048608 | tf_op jit(solution)/shard_map/ppermute | solution.py:14
  357.6 11.6 %collective-permute-start.5 = (f32[512,512]{0,1:T(8,128)S(1)}, f32[512,512]{0,1:T(8,128)}, u32[]{:S(2)}, u32[]{:S(2)}) collective-permute-start(f32[512,512]{0,1:T(8,128)S(1)} %add.101), channel_id=1, source_target_pairs={{0,64},{8,72},{16,80},{24,88},{32,96},{40,104},{48,112},{56,120},{... | collective-permute-start | bytes 3145736 | tf_op jit(solution)/shard_map/ppermute | solution.py:14
  369.3 44.7 %collective-permute-done.5 = f32[512,512]{0,1:T(8,128)} collective-permute-done((f32[512,512]{0,1:T(8,128)S(1)}, f32[512,512]{0,1:T(8,128)}, u32[]{:S(2)}, u32[]{:S(2)}) %collective-permute-start.5) | collective-permute-done | bytes 1048608 | tf_op jit(solution)/shard_map/ppermute | solution.py:14
  419.5 11.7 %cholesky.104 = f32[128,128]{1,0:T(8,128)S(1)} custom-call(f32[128,128]{1,0:T(8,128)S(1)} %cholesky.266), custom_call_target="Cholesky" | custom-call | tf_op jit(solution)/shard_map/jit(cholesky)/cholesky | solution.py:34
  431.4 9.8 %custom-call.31 = f32[1,128,128]{1,2,0:T(8,128)S(1)} custom-call(f32[1,128,128]{2,1,0:T(8,128)S(1)} %get-tuple-element.41), custom_call_target="InvertDiagBlocksLowerTriangular" | custom-call | tf_op jit(solution)/shard_map/jit(cholesky)/cholesky | solution.py:34
  443.7 11.7 %cholesky.217 = f32[128,128]{1,0:T(8,128)S(1)} custom-call(f32[128,128]{1,0:T(8,128)S(1)} %cholesky.270), custom_call_target="Cholesky" | custom-call | tf_op jit(solution)/shard_map/jit(cholesky)/cholesky | solution.py:34
  455.4 10.0 %custom-call.32 = f32[1,128,128]{1,2,0:T(8,128)S(1)} custom-call(f32[1,128,128]{2,1,0:T(8,128)S(1)} %get-tuple-element.38), custom_call_target="InvertDiagBlocksLowerTriangular" | custom-call | tf_op jit(solution)/shard_map/jit(cholesky)/cholesky | solution.py:34
  467.0 11.7 %cholesky.238 = f32[128,128]{1,0:T(8,128)S(1)} custom-call(f32[128,128]{1,0:T(8,128)S(1)} %cholesky.275), custom_call_target="Cholesky" | custom-call | tf_op jit(solution)/shard_map/jit(cholesky)/cholesky | solution.py:34
  479.4 11.3 %custom-call.33 = f32[1,128,128]{1,2,0:T(8,128)} custom-call(f32[1,128,128]{2,1,0:T(8,128)} %get-tuple-element.35), custom_call_target="InvertDiagBlocksLowerTriangular" | custom-call | tf_op jit(solution)/shard_map/jit(cholesky)/cholesky | solution.py:34
  493.0 11.7 %cholesky.255 = f32[128,128]{1,0:T(8,128)S(1)} custom-call(f32[128,128]{1,0:T(8,128)S(1)} %slice_subtract_fusion.2), custom_call_target="Cholesky" | custom-call | tf_op jit(solution)/shard_map/jit(cholesky)/cholesky | solution.py:34
  510.6 14.0 %while.1 = (s32[]{:T(128)}, f32[512,512]{1,0:T(8,128)}, s32[4,2]{0,1:T(2,128)S(1)}, f32[4,128,128]{2,1,0:T(8,128)}, s32[]{:T(128)}) while((s32[]{:T(128)}, f32[512,512]{1,0:T(8,128)}, s32[4,2]{0,1:T(2,128)S(1)}, f32[4,128,128]{2,1,0:T(8,128)}, s32[]{:T(128)}) %tuple.37), condition=%wide.while_cond, body=%wide.while_body.sunk | while | flops 2 | bytes 132205 | solution.py:35
  511.2 2.9 bitcast_dynamic-update-slice_fusion.2
  514.8 2.9 bitcast_dynamic-update-slice_fusion.2
  518.3 2.9 bitcast_dynamic-update-slice_fusion.2
  521.8 2.9 bitcast_dynamic-update-slice_fusion.2
  524.7 40.8 %custom-call.34 = f32[4,128,128]{1,2,0:T(8,128)} custom-call(f32[4,128,128]{2,1,0:T(8,128)} %get-tuple-element.11), custom_call_target="InvertDiagBlocksLowerTriangular" | custom-call | tf_op jit(solution)/shard_map/jit(_solve_triangular)/triangular_solve | solution.py:35
  577.2 99.6 %reduce-scatter.2.cloned.1.call-done = f32[32,1792]{1,0:T(8,128)} async-done(((f32[512,1792]{1,0:T(8,128)}), f32[32,1792]{1,0:T(8,128)}) %reduce-scatter.2.cloned.1.call-update) | async-done | bytes 229392 | tf_op jit(solution)/shard_map/reduce_scatter | solution.py:66
  677.9 12.4 %psum.15 = f32[32]{0:T(128)S(1)} all-reduce(f32[32]{0:T(128)S(1)} %multiply_reduce_fusion), channel_id=1, replica_groups=mesh['rep'=4,'fsdp'=16,'tp'=8] {'tp'}, use_global_device_ids=true, to_apply=%region_13.14 | all-reduce | flops 32 | bytes 256 | tf_op jit(solution)/shard_map/psum | solution.py:67
  693.1 67.5 %all-gather.5.cloned.1.call-done = bf16[512,1792]{1,0:T(8,128)(2,1)} async-done(((bf16[32,1792]{1,0:T(8,128)(2,1)}), bf16[512,1792]{1,0:T(8,128)(2,1)}) %all-gather.5.cloned.1.call-update) | async-done | bytes 1835024 | tf_op jit(solution)/shard_map/all_gather | solution.py:74
  760.6 3.1 fusion.2
  (80 shorter events, 43.0 us)
Async XLA Ops:
  7.2 80.3 %all-gather.3.cloned.1.call-start = ((), (), s32[]{:S(2)}) async-start(), calls=%async_computation.1 | async-start | bytes 1949696 | tf_op jit(solution)/shard_map/all_gather | solution.py:56
  7.9 155.7 %all-reduce.3.cloned.1.call-start = ((), (), s32[]{:S(2)}) async-start(), calls=%async_computation.2 | async-start | bytes 1048576 | tf_op jit(solution)/shard_map/psum | solution.py:58
  7.9 24.2 %collective-permute-start.1 = (bf16[1,256,1792]{2,1,0:T(8,128)(2,1)}, bf16[1,256,1792]{2,1,0:T(8,128)(2,1)S(1)}, u32[]{:S(2)}, u32[]{:S(2)}) collective-permute-start(bf16[1,256,1792]{2,1,0:T(8,128)(2,1)} %param.5), channel_id=1, source_target_pairs={{128,0},{256,128},{384,256},{0,384},{129,1},{257,129},{385,257},{1... | collective-permute-start | bytes 2752520 | tf_op jit(solution)/shard_map/ppermute | solution.py:28
  15.8 19.6 %collective-permute-start = (bf16[1,256,1792]{2,1,0:T(8,128)(2,1)}, bf16[1,256,1792]{2,1,0:T(8,128)(2,1)S(1)}, u32[]{:S(2)}, u32[]{:S(2)}) collective-permute-start(bf16[1,256,1792]{2,1,0:T(8,128)(2,1)} %param.5), channel_id=1, source_target_pairs={{0,128},{128,256},{256,384},{384,0},{1,129},{129,257},{257,385},{3... | collective-permute-start | bytes 2752520 | tf_op jit(solution)/shard_map/ppermute | solution.py:25
  32.1 3.2 copy-start.7
  35.3 0.9 copy-start.8
  36.3 51.2 %copy-start = (bf16[1,256,1792]{2,1,0:T(8,128)(2,1)S(1)}, bf16[1,256,1792]{2,1,0:T(8,128)(2,1)}, u32[]{:S(2)}) copy-start(bf16[1,256,1792]{2,1,0:T(8,128)(2,1)} %param.7) | copy-start | bytes 2752516
  90.5 586.4 %reduce-scatter.2.cloned.1.call-start = ((), (), s32[]{:S(2)}) async-start(), calls=%async_computation.3 | async-start | bytes 3899392 | tf_op jit(solution)/shard_map/reduce_scatter | solution.py:66
  165.8 24.8 %collective-permute-start.2 = (f32[512,512]{0,1:T(8,128)S(1)}, f32[512,512]{0,1:T(8,128)S(1)}, u32[]{:S(2)}, u32[]{:S(2)}) collective-permute-start(f32[512,512]{0,1:T(8,128)S(1)} %fusion.52), channel_id=1, source_target_pairs={{0,8},{8,0},{16,24},{24,16},{32,40},{40,32},{48,56},{56,48},{64,72... | collective-permute-start | bytes 3145736 | tf_op jit(solution)/shard_map/ppermute | solution.py:14
  190.8 47.2 %collective-permute-start.3 = (f32[512,512]{0,1:T(8,128)S(1)}, f32[512,512]{0,1:T(8,128)S(1)}, u32[]{:S(2)}, u32[]{:S(2)}) collective-permute-start(f32[512,512]{0,1:T(8,128)S(1)} %add.99), channel_id=1, source_target_pairs={{0,16},{8,24},{16,0},{24,8},{32,48},{40,56},{48,32},{56,40},{64,80... | collective-permute-start | bytes 3145736 | tf_op jit(solution)/shard_map/ppermute | solution.py:14
  238.2 119.2 %collective-permute-start.4 = (f32[512,512]{0,1:T(8,128)S(1)}, f32[512,512]{0,1:T(8,128)S(1)}, u32[]{:S(2)}, u32[]{:S(2)}) collective-permute-start(f32[512,512]{0,1:T(8,128)S(1)} %add.100), channel_id=1, source_target_pairs={{0,32},{8,40},{16,48},{24,56},{32,0},{40,8},{48,16},{56,24},{64,96... | collective-permute-start | bytes 3145736 | tf_op jit(solution)/shard_map/ppermute | solution.py:14
  357.6 11.6 %copy-start.3 = (f32[512,512]{0,1:T(8,128)}, f32[512,512]{0,1:T(8,128)S(1)}, u32[]{:S(2)}) copy-start(f32[512,512]{0,1:T(8,128)S(1)} %add.101) | copy-start | bytes 3145732
  357.6 56.3 %collective-permute-start.5 = (f32[512,512]{0,1:T(8,128)S(1)}, f32[512,512]{0,1:T(8,128)}, u32[]{:S(2)}, u32[]{:S(2)}) collective-permute-start(f32[512,512]{0,1:T(8,128)S(1)} %add.101), channel_id=1, source_target_pairs={{0,64},{8,72},{16,80},{24,88},{32,96},{40,104},{48,112},{56,120},{... | collective-permute-start | bytes 3145736 | tf_op jit(solution)/shard_map/ppermute | solution.py:14
  418.5 1.0 copy-start.6
  479.4 86.1 %copy-start.2 = (f32[256,512]{1,0:T(8,128)S(1)}, f32[256,512]{1,0:T(8,128)}, u32[]{:S(2)}) copy-start(f32[256,512]{1,0:T(8,128)} %all-reduce.3.cloned.1.call-done) | copy-start | bytes 1572868
  524.7 50.0 %copy-start.1 = (bf16[1,256,1792]{2,1,0:T(8,128)(2,1)S(1)}, bf16[1,256,1792]{2,1,0:T(8,128)(2,1)}, u32[]{:S(2)}) copy-start(bf16[1,256,1792]{2,1,0:T(8,128)(2,1)} %param.7) | copy-start | bytes 2752516
  571.7 3.0 copy-start.4
  577.2 115.0 %copy-start.5 = (f32[128,256]{1,0:T(8,128)S(1)}, f32[128,256]{1,0:T(8,128)}, u32[]{:S(2)}) copy-start(f32[128,256]{1,0:T(8,128)} %copy-done.4) | copy-start | bytes 393220
  577.2 183.4 %all-gather.5.cloned.1.call-start = ((), (), s32[]{:S(2)}) async-start(), calls=%async_computation.4 | async-start | bytes 1949696 | tf_op jit(solution)/shard_map/all_gather | solution.py:74
Sparse Core Ops, SparseCore 0:
  10.1 77.3 all-gather.2
  90.6 72.8 all-reduce.2
  577.3 99.5 reduce-scatter.1
  692.3 68.2 all-gather.4
